TPU v7x, 32 devices: a whole 2x2x4 slice. The times are simulated.
32 devices in a mesh: dp: 8 (over z, y), tp: 4 (over x, core).
Axes of the slice: x: 2, y: 2, z: 4, core: 2. Of those that a mesh axis runs over, the one named last changes fastest.
Arguments:
- tokens: bfloat16 [8, 2048, 768], P('dp', 'tp'), may hold values from -6 to 6
- cotangent: bfloat16 [8, 2048, 768], P('dp', 'tp'), may hold values from -6 to 6
- tags: int32 [8], P('dp'), may hold values from 0 to 7
- tag_weight: float32 [8], replicated, may hold values from 0.25 to 4
- query_weight: bfloat16 [768, 768], P(None, 'tp'), may hold values from -0.21875 to 0.21875
- key_value_weight: bfloat16 [768, 128], replicated, may hold values from -0.21875 to 0.21875
- output_weight: bfloat16 [768, 768], P('tp'), may hold values from -1.25 to 1.25
- up_weight: bfloat16 [768, 3072], P(None, 'tp'), may hold values from -0.21875 to 0.21875
- down_weight: bfloat16 [3072, 768], P('tp'), may hold values from -0.109375 to 0.109375
- norm_gain_one: float32 [768], replicated, may hold values from 0.25 to 1.75
- norm_bias_one: float32 [768], replicated, may hold values from -1.5 to 1.5
- norm_gain_two: float32 [768], replicated, may hold values from 0.25 to 1.75
- norm_bias_two: float32 [768], replicated, may hold values from -1.5 to 1.5
Outputs:
- block_out: bfloat16 [8, 2048, 768], P('dp', 'tp')
- grad_tokens: bfloat16 [8, 2048, 768], P('dp', 'tp')
- grad_query: float32 [768, 768], P(None, 'tp')
- grad_keyval: float32 [768, 128], replicated
- grad_output: float32 [768, 768], P('tp')
- grad_upward: float32 [768, 3072], P(None, 'tp')
- grad_downward: float32 [3072, 768], P('tp')
- grad_gain_one: float32 [768], replicated
- grad_bias_one: float32 [768], replicated
- grad_gain_two: float32 [768], replicated
- grad_bias_two: float32 [768], replicated
All inputs are finite; a program needn't handle non-finite values.
Results may differ from a plain program's by a relative error of at most 0.013.
Values may be sent and summed in bfloat16 or wider, within the bound.
A program may use at most 128 MiB of HBM per device.

v0:
```python
import jax
import jax.numpy as jnp
from jax import lax
from jax.sharding import PartitionSpec as P

HD = 64
ROT = 16


def layer_norm(values, gain_vec, shift_vec):
    row_mean = jnp.mean(values, axis=-1, keepdims=True)
    centred = values - row_mean
    variance = jnp.mean(centred * centred, axis=-1, keepdims=True)
    inverse = lax.rsqrt(variance + 1e-05)
    normal = centred * inverse
    return (normal * gain_vec + shift_vec, normal, inverse)


def norm_back(upstream, normal, inverse, gain_vec):
    scaled = upstream * gain_vec
    term_one = jnp.mean(scaled, axis=-1, keepdims=True)
    term_two = jnp.mean(scaled * normal, axis=-1, keepdims=True)
    return inverse * (scaled - term_one - normal * term_two)


def rot_angles(positions):
    frequencies = 10000.0 ** (-jnp.arange(0, ROT, 2, dtype=jnp.float32) / ROT)
    return positions.astype(jnp.float32)[:, None] * frequencies[None, :]


def rotate(values, angles, direction):
    half_rot = ROT // 2
    cosine = jnp.cos(angles)[:, None, :]
    sine_part = direction * jnp.sin(angles)[:, None, :]
    front_half = values[..., :half_rot]
    back_half = values[..., half_rot:ROT]
    return jnp.concatenate(
        [
            front_half * cosine - back_half * sine_part,
            back_half * cosine + front_half * sine_part,
            values[..., ROT:],
        ],
        axis=-1,
    )


def outer_sum(left, right):
    return lax.dot_general(
        left, right, (((0, 1), (0, 1)), ((), ())), preferred_element_type=jnp.float32
    )


def against(left, weight):
    return lax.dot_general(
        left, weight, (((2,), (1,)), ((), ())), preferred_element_type=jnp.float32
    )


def shards(
    tokens,
    cotangent,
    tags,
    tag_weight,
    query_weight,
    key_value_weight,
    output_weight,
    up_weight,
    down_weight,
    norm_gain_one,
    norm_bias_one,
    norm_gain_two,
    norm_bias_two,
):
    seq_dev, own_len, model_width = tokens.shape
    full_len = own_len * lax.axis_size("tp")
    heads_dev = query_weight.shape[1] // HD
    score_scale = HD ** (-0.5)
    block_rows = min(512, full_len)
    blocks = full_len // block_rows
    own_rows = tokens.astype(jnp.float32)
    full_angles = rot_angles(jnp.arange(full_len))
    first_normed, normal_one, inverse_one = layer_norm(own_rows, norm_gain_one, norm_bias_one)
    second_normed, normal_two, inverse_two = layer_norm(own_rows, norm_gain_two, norm_bias_two)
    low_one = first_normed.astype(jnp.bfloat16)
    low_two = second_normed.astype(jnp.bfloat16)
    rows_one, rows_two = (
        lax.all_gather(low_one, "tp", axis=1, tiled=True),
        lax.all_gather(low_two, "tp", axis=1, tiled=True),
    )
    key_value_rows = jnp.dot(rows_one, key_value_weight, preferred_element_type=jnp.float32)
    key_part = rotate(key_value_rows[:, :, None, :HD], full_angles, 1.0)[:, :, 0, :]
    key_value_rows = jnp.concatenate([key_part, key_value_rows[:, :, HD:]], axis=-1).astype(
        jnp.bfloat16
    )
    key_rows = key_value_rows[:, :, :HD]
    value_rows = key_value_rows[:, :, HD:]
    query_matrix = jnp.dot(rows_one, query_weight, preferred_element_type=jnp.float32).reshape(
        seq_dev, full_len, heads_dev, HD
    )
    query_matrix = rotate(query_matrix, full_angles, 1.0).astype(jnp.bfloat16)

    def block_scores(query_block, block_start):
        block_end = block_start + block_rows
        scores = (
            jnp.einsum(
                "sqhd,skd->sqhk",
                query_block,
                key_rows[:, :block_end],
                preferred_element_type=jnp.float32,
            )
            * score_scale
        )
        allowed = jnp.arange(block_end)[None, :] <= (block_start + jnp.arange(block_rows))[:, None]
        return jnp.where(allowed[None, :, None, :], scores, -1e30)

    context_list = []
    lse_list = []
    for block_index in range(blocks):
        block_start = block_index * block_rows
        block_end = block_start + block_rows
        scores = block_scores(query_matrix[:, block_start:block_end], block_start)
        row_top = jnp.max(scores, axis=-1, keepdims=True)
        weights = jnp.exp(scores - row_top)
        row_total = jnp.sum(weights, axis=-1, keepdims=True)
        weights_low = (weights / row_total).astype(jnp.bfloat16)
        context_list.append(
            jnp.einsum(
                "sqhk,skd->sqhd",
                weights_low,
                value_rows[:, :block_end],
                preferred_element_type=jnp.float32,
            )
        )
        lse_list.append(row_top + jnp.log(row_total))
    context_full = jnp.concatenate(context_list, axis=1)
    low_context = context_full.reshape(seq_dev, full_len, heads_dev * HD).astype(jnp.bfloat16)
    attention_branch = jnp.dot(low_context, output_weight, preferred_element_type=jnp.float32)
    hidden_rows = jnp.dot(rows_two, up_weight, preferred_element_type=jnp.float32)
    middle_rows = jax.nn.gelu(hidden_rows, approximate=False).astype(jnp.bfloat16)
    feedforward_branch = jnp.dot(middle_rows, down_weight, preferred_element_type=jnp.float32)
    branch = lax.psum_scatter(
        (attention_branch + feedforward_branch).astype(jnp.bfloat16),
        "tp",
        scatter_dimension=1,
        tiled=True,
    ).astype(jnp.float32)
    block_out = (own_rows + branch).astype(jnp.bfloat16)
    tag_ids = jnp.arange(tag_weight.shape[0], dtype=jnp.int32)
    row_weight = jnp.sum(
        jnp.where(tags[:, None] == tag_ids[None, :], tag_weight[None, :], 0.0), axis=1
    )
    upstream = cotangent.astype(jnp.float32) * row_weight[:, None, None]
    grad_rows = lax.all_gather(upstream.astype(jnp.bfloat16), "tp", axis=1, tiled=True)
    grad_output = outer_sum(low_context, grad_rows)
    grad_downward = outer_sum(middle_rows, grad_rows)
    grad_context = (
        against(grad_rows, output_weight)
        .astype(jnp.bfloat16)
        .reshape(seq_dev, full_len, heads_dev, HD)
    )
    grad_middle = against(grad_rows, down_weight)
    normal_cdf = 0.5 * (1.0 + lax.erf(hidden_rows * 0.7071067811865476))
    density = jnp.exp(-0.5 * hidden_rows * hidden_rows) * 0.3989422804014327
    grad_hidden = (grad_middle * (normal_cdf + hidden_rows * density)).astype(jnp.bfloat16)
    grad_upward = outer_sum(rows_two, grad_hidden)
    norm_part_two = against(grad_hidden, up_weight)
    grad_kv_full = jnp.zeros((seq_dev, full_len, 2 * HD), jnp.float32)
    query_grad_list = []
    for block_index in range(blocks):
        block_start = block_index * block_rows
        block_end = block_start + block_rows
        query_block = query_matrix[:, block_start:block_end]
        grad_block = grad_context[:, block_start:block_end]
        scores = block_scores(query_block, block_start)
        weights = jnp.exp(scores - lse_list[block_index])
        grad_weights = jnp.einsum(
            "sqhd,skd->sqhk",
            grad_block,
            value_rows[:, :block_end],
            preferred_element_type=jnp.float32,
        )
        row_delta = jnp.sum(
            grad_block.astype(jnp.float32) * context_list[block_index], axis=-1, keepdims=True
        )
        grad_scores = (weights * (grad_weights - row_delta)).astype(jnp.bfloat16)
        query_grad_list.append(
            jnp.einsum(
                "sqhk,skd->sqhd",
                grad_scores,
                key_rows[:, :block_end],
                preferred_element_type=jnp.float32,
            )
            * score_scale
        )
        grad_keys = (
            jnp.einsum(
                "sqhk,sqhd->skd", grad_scores, query_block, preferred_element_type=jnp.float32
            )
            * score_scale
        )
        grad_values = jnp.einsum(
            "sqhk,sqhd->skd",
            weights.astype(jnp.bfloat16),
            grad_block,
            preferred_element_type=jnp.float32,
        )
        grad_kv_full = grad_kv_full.at[:, :block_end].add(
            jnp.concatenate([grad_keys, grad_values], axis=-1)
        )
    grad_queries = jnp.concatenate(query_grad_list, axis=1)
    grad_queries = (
        rotate(grad_queries, full_angles, -1.0)
        .reshape(seq_dev, full_len, heads_dev * HD)
        .astype(jnp.bfloat16)
    )
    grad_query = outer_sum(rows_one, grad_queries)
    norm_part_one = against(grad_queries, query_weight)
    key_back = rotate(grad_kv_full[:, :, None, :HD], full_angles, -1.0)[:, :, 0, :]
    keyval_part = jnp.concatenate([key_back, grad_kv_full[:, :, HD:]], axis=-1)
    sum_one, sum_two, sum_keyval = (
        lax.psum_scatter(
            norm_part_one.astype(jnp.bfloat16), "tp", scatter_dimension=1, tiled=True
        ).astype(jnp.float32),
        lax.psum_scatter(
            norm_part_two.astype(jnp.bfloat16), "tp", scatter_dimension=1, tiled=True
        ).astype(jnp.float32),
        lax.psum_scatter(
            keyval_part.astype(jnp.bfloat16), "tp", scatter_dimension=1, tiled=True
        ).astype(jnp.float32),
    )
    low_keyval = sum_keyval.astype(jnp.bfloat16)
    grad_keyval = outer_sum(low_one, low_keyval)
    upstream_one = sum_one + against(low_keyval, key_value_weight)
    grad_gain_one = jnp.sum(upstream_one * normal_one, axis=(0, 1))
    grad_bias_one = jnp.sum(upstream_one, axis=(0, 1))
    grad_gain_two = jnp.sum(sum_two * normal_two, axis=(0, 1))
    grad_bias_two = jnp.sum(sum_two, axis=(0, 1))
    grad_tokens = (
        upstream
        + norm_back(upstream_one, normal_one, inverse_one, norm_gain_one)
        + norm_back(sum_two, normal_two, inverse_two, norm_gain_two)
    )
    grad_query, grad_output, grad_upward, grad_downward = lax.psum(
        (grad_query, grad_output, grad_upward, grad_downward), "dp"
    )
    grad_keyval, grad_gain_one, grad_bias_one, grad_gain_two, grad_bias_two = lax.psum(
        (grad_keyval, grad_gain_one, grad_bias_one, grad_gain_two, grad_bias_two), ("dp", "tp")
    )
    return (
        block_out,
        grad_tokens.astype(jnp.bfloat16),
        grad_query,
        grad_keyval,
        grad_output,
        grad_upward,
        grad_downward,
        grad_gain_one,
        grad_bias_one,
        grad_gain_two,
        grad_bias_two,
    )


def solution(mesh):
    in_specs = (
        P("dp", "tp", None),
        P("dp", "tp", None),
        P("dp"),
        P(),
        P(None, "tp"),
        P(),
        P("tp", None),
        P(None, "tp"),
        P("tp", None),
        P(),
        P(),
        P(),
        P(),
    )
    out_specs = (
        P("dp", "tp", None),
        P("dp", "tp", None),
        P(None, "tp"),
        P(),
        P("tp", None),
        P(None, "tp"),
        P("tp", None),
        P(),
        P(),
        P(),
        P(),
    )
    return jax.shard_map(shards, mesh=mesh, in_specs=in_specs, out_specs=out_specs, check_vma=False)
```

profile of v0, /device:TPU:0, one launch (start us, length us, event | category | flops | bytes accessed | tf_op | source)
XLA Modules:
  0.0 634.0 jit_solution(16872320583740692377)
XLA Ops:
  7.3 1.4 convert_reduce_fusion.1
  8.7 1.5 fusion.101
  10.2 2.9 fusion.89
  14.5 1.6 fusion.110
  16.9 0.8 iota_compare_fusion.5
  18.1 1.4 iota_compare_fusion.1
  20.2 0.9 broadcast_multiply_fusion
  21.1 23.4 %all-gather.4.cloned.1.call-done = bf16[1,2048,768]{2,1,0:T(8,128)(2,1)} async-done(((bf16[1,512,768]{2,1,0:T(8,128)(2,1)}), bf16[1,2048,768]{2,1,0:T(8,128)(2,1)}) %all-gather.4.cloned.1.call-update) | async-done | bytes 3145744 | tf_op jit(solution)/shard_map/all_gather | solution.py:87
  44.5 3.2 fusion.186
  48.2 2.1 fusion.58
  50.6 1.3 fusion.31
  51.9 2.1 fusion.25
  54.6 2.9 fusion.190
  57.5 2.0 fusion.187
  59.5 1.4 fusion.2
  60.9 2.2 copy-done.1
  63.1 2.8 fusion.189
  66.5 5.9 fusion.4
  72.3 6.7 %fusion = f32[512,3]{0,1:T(4,128)S(1)} fusion(f32[512,3,2048]{2,0,1:T(8,128)} %get-tuple-element.114, f32[512,3]{0,1:T(4,128)S(1)} %get-tuple-element.113, pred[512,2048]{1,0:T(8,128)(4,1)S(1)} %iota_compare_fusion), kind=kLoop, calls=%fused_computation.5 | loop fusion | flops 12581376 | bytes 13643776 | tf_op jit(solution)/shard_map/reduce_sum | solution.py:124
  79.1 7.8 %fusion.188 = (bf16[512,3,64]{0,2,1:T(8,128)(2,1)}, f32[512,3,64]{0,2,1:T(8,128)}) fusion(bf16[1,2048,128]{1,2,0:T(8,128)(2,1)S(1)} %get-tuple-element.107, f32[512,3,2048]{2,0,1:T(8,128)} %get-tuple-element.114, f32[512,3]{0,1:T(4,128)S(1)} %fusion, f32[512,3]{0,1:T(4,128)S(1)} %get-tuple-element.113, pred[512,2048]{1,0:T(8,128)(4,1)S(1)} %iota_compare_fusion), kind=kOutput, calls=%fused_computation.286 | convolution fusion | flops 418480128 | bytes 14499840 | tf_op jit(solution)/shard_map/sqhk,skd->sqhd/dot_general | solution.py:127
  88.2 1.6 copy-done.3
  91.0 3.2 fusion.61
  94.9 1.4 fusion.133
  96.4 0.8 multiply_convert_fusion.3
  97.2 1.1 copy-done.7
  99.0 1.9 fusion.116
  100.9 2.4 multiply_convert_fusion.2
  104.0 0.8 copy-done.6
  104.9 2.1 multiply_convert_fusion.1
  107.0 8.8 %multiply_convert_fusion = bf16[512,3,2048]{2,0,1:T(8,128)(2,1)S(1)} fusion(f32[512,3,2048]{2,0,1:T(8,128)} %get-tuple-element.114, f32[512,3]{0,1:T(4,128)S(1)} %get-tuple-element.80, f32[512,3]{0,1:T(4,128)S(1)} %copy-done.48, pred[512,2048]{1,0:T(8,128)(4,1)S(1)} %iota_compare_fusion, bf16[1,2048,128]{1,2,0:T(8,128)(2,1)S(1)} %copy-done.20, ...), kind=kOutput, calls=%fused_computation | convolution fusion | flops 421527552 | bytes 20398080 | tf_op jit(solution)/shard_map/sqhd,skd->sqhk/dot_general | solution.py:176
  116.1 0.9 fusion.76
  117.0 1.2 fusion.74
  118.5 1.6 fusion.67
  120.3 6.4 %fusion.70 = f32[1,2048,64]{1,2,0:T(8,128)S(1)} fusion(f32[512,3,2048]{2,0,1:T(8,128)} %get-tuple-element.114, f32[512,3]{0,1:T(4,128)S(1)} %copy-done.48, pred[512,2048]{1,0:T(8,128)(4,1)S(1)} %iota_compare_fusion, bf16[1,2048,3,64]{1,3,2,0:T(8,128)(2,1)S(1)} %bitcast.283), kind=kOutput, calls=%fused_computation.100 | convolution fusion | flops 415236096 | bytes 14360576 | tf_op jit(solution)/shard_map/sqhk,sqhd->skd/dot_general | solution.py:201
  127.8 0.8 pad_maximum_fusion.2
  128.7 17.5 %fusion.7 = (bf16[2048,768]{1,0:T(8,128)(2,1)}, f32[2048,768]{1,0:T(8,128)S(1)}) fusion(bf16[768,768]{1,0:T(8,128)(2,1)S(1)} %copy-done, bf16[1,2048,768]{2,1,0:T(8,128)(2,1)} %all-gather.6.cloned.1.call-done), kind=kOutput, calls=%fused_computation.19 | convolution fusion | flops 2518155264 | bytes 13762560 | tf_op jit(solution)/shard_map/dot_general | solution.py:138
  146.3 5.2 fusion.13
  151.5 1.7 copy-done.59
  153.2 4.0 fusion.54
  157.5 1.9 fusion.113
  159.5 3.1 fusion.112
  162.7 4.0 fusion.115
  166.7 2.0 fusion.114
  169.0 2.7 fusion.53
  171.8 4.9 fusion.191
  176.8 2.7 fusion.55
  179.8 3.6 fusion.34
  183.6 4.2 fusion.39
  187.8 4.2 fusion.32
  192.0 2.1 fusion.127
  194.2 3.6 fusion.47
  197.9 37.9 %reduce-scatter.7.cloned.1.call-done = bf16[1,512,768]{2,1,0:T(8,128)(2,1)} async-done(((bf16[1,2048,768]{2,1,0:T(8,128)(2,1)}), bf16[1,512,768]{2,1,0:T(8,128)(2,1)}) %reduce-scatter.7.cloned.1.call-update) | async-done | bytes 786448 | tf_op jit(solution)/shard_map/reduce_scatter | solution.py:221
  235.8 4.6 fusion.100
  240.4 40.1 %all-reduce.1 = (f32[768]{0:T(1024)}, f32[768]{0:T(1024)}, f32[768]{0:T(1024)}, f32[768]{0:T(1024)}) all-reduce(f32[768]{0:T(1024)} %get-tuple-element.67, f32[768]{0:T(1024)} %get-tuple-element.72, f32[768]{0:T(1024)} %get-tuple-element.74, f32[768]{0:T(1024)} %get-tuple-element.76), channel_id=1, replica_groups=mesh['dp'=8,'tp'=4] {'dp','tp'}, use_global_device_ids=true, to_apply=%region_29.30 | all-reduce | flops 3072 | bytes 24576 | tf_op jit(solution)/shard_map/psum | solution.py:246
  280.5 1.2 broadcast_multiply_fusion.1
  281.7 1.3 broadcast_multiply_fusion.3
  283.0 4.0 fusion.97
  287.0 122.9 %all-reduce.6.cloned.1.call-done = f32[768,128]{1,0:T(8,128)} async-done(((f32[768,128]{1,0:T(8,128)}), f32[768,128]{1,0:T(8,128)}) %all-reduce.6.cloned.1.call-update) | async-done | bytes 393232 | tf_op jit(solution)/shard_map/psum | solution.py:246
  410.0 206.7 %all-reduce.8.cloned.1.call-done = (f32[768,192]{0,1:T(8,128)}, f32[192,768]{1,0:T(8,128)}, f32[768,768]{1,0:T(8,128)}, f32[768,768]{1,0:T(8,128)}) async-done(((f32[768,192]{0,1:T(8,128)}, f32[192,768]{1,0:T(8,128)}, f32[768,768]{1,0:T(8,128)}, f32[768,768]{1,0:T(8,128)}), (f32[768,192]{0,1:T(8,128)}, f32[192,768]{1,0:T(8,128)}, f32[768,768]{1,0:T(8,128)}, ...) | async-done | bytes 5898256 | tf_op jit(solution)/shard_map/psum | solution.py:243
  616.7 2.1 copy.42
  618.7 1.8 copy.43
  620.5 1.9 copy.44
  622.4 3.2 copy.45
  625.6 1.4 copy.46
  (201 shorter events, 11.8 us)
Async XLA Ops:
  7.2 121.6 %copy-start = (bf16[768,768]{1,0:T(8,128)(2,1)S(1)}, bf16[768,768]{1,0:T(8,128)(2,1)}, u32[]{:S(2)}) copy-start(bf16[768,768]{1,0:T(8,128)(2,1)} %param.30) | copy-start | bytes 3538948
  7.2 6.6 %copy-start.57 = (f32[8]{0:T(128)S(1)}, f32[8]{0:T(128)}, u32[]{:S(2)}) copy-start(f32[8]{0:T(128)} %param.26) | copy-start | bytes 100
  7.2 7.3 %copy-start.12 = (bf16[1,512,768]{2,1,0:T(8,128)(2,1)S(1)}, bf16[1,512,768]{2,1,0:T(8,128)(2,1)}, u32[]{:S(2)}) copy-start(bf16[1,512,768]{2,1,0:T(8,128)(2,1)} %param.24) | copy-start | bytes 2359300
  7.2 37.3 %all-gather.4.cloned.1.call-start = ((), (), s32[]{:S(2)}) async-start(), calls=%async_computation.4 | async-start | bytes 3932160 | tf_op jit(solution)/shard_map/all_gather | solution.py:87
  8.7 9.4 %copy-start.38 = (f32[512]{0:T(512)}, f32[512]{0:T(512)S(1)}, u32[]{:S(2)}) copy-start(f32[512]{0:T(512)S(1)} %broadcast_multiply_fusion.5) | copy-start | bytes 6148
  10.2 34.3 %copy-start.32 = (bf16[768,128]{1,0:T(8,128)(2,1)S(1)}, bf16[768,128]{1,0:T(8,128)(2,1)}, u32[]{:S(2)}) copy-start(bf16[768,128]{1,0:T(8,128)(2,1)} %param.28) | copy-start | bytes 589828
  10.2 7.9 %copy-start.44 = (f32[512]{0:T(512)}, f32[512]{0:T(512)S(1)}, u32[]{:S(2)}) copy-start(f32[512]{0:T(512)S(1)} %add_rsqrt_fusion) | copy-start | bytes 6148
  13.1 77.8 %all-gather.8.cloned.1.call-start = ((), (), s32[]{:S(2)}) async-start(), calls=%async_computation.7 | async-start | bytes 3932160 | tf_op jit(solution)/shard_map/all_gather | solution.py:153
  16.1 112.6 %all-gather.6.cloned.1.call-start = ((), (), s32[]{:S(2)}) async-start(), calls=%async_computation.5 | async-start | bytes 3932160 | tf_op jit(solution)/shard_map/all_gather | solution.py:88
  16.8 175.2 %reduce-scatter.9.cloned.1.call-start = ((), (), s32[]{:S(2)}) async-start(), calls=%async_computation.9 | async-start | bytes 655360 | tf_op jit(solution)/shard_map/reduce_scatter | solution.py:227
  16.9 33.4 %copy-start.50 = (f32[8]{0:T(128)}, f32[8]{0:T(128)S(1)}, u32[]{:S(2)}) copy-start(f32[8]{0:T(128)S(1)} %multiply_power_fusion) | copy-start | bytes 100
  21.1 29.3 %copy-start.21 = (f32[2048,8]{0,1:T(8,128)}, f32[2048,8]{0,1:T(8,128)S(1)}, u32[]{:S(2)}) copy-start(f32[2048,8]{0,1:T(8,128)S(1)} %get-tuple-element.104) | copy-start | bytes 196612
  44.5 3.6 copy-start.8
  47.7 31.4 %copy-start.19 = (bf16[1,2048,128]{1,2,0:T(8,128)(2,1)}, bf16[1,2048,128]{1,2,0:T(8,128)(2,1)S(1)}, u32[]{:S(2)}) copy-start(bf16[1,2048,128]{1,2,0:T(8,128)(2,1)S(1)} %get-tuple-element.107) | copy-start | bytes 1572868
  47.8 18.7 %copy-start.15 = (bf16[1,2048,1,48]{1,3,2,0:T(8,128)(2,1)}, bf16[1,2048,1,48]{1,3,2,0:T(8,128)(2,1)S(1)}, u32[]{:S(2)}) copy-start(bf16[1,2048,1,48]{1,3,2,0:T(8,128)(2,1)S(1)} %slice.370) | copy-start | bytes 589828
  48.1 18.3 %copy-start.26 = (bf16[1,2048,1,8]{1,3,2,0:T(8,128)(2,1)}, bf16[1,2048,1,8]{1,3,2,0:T(8,128)(2,1)S(1)}, u32[]{:S(2)}) copy-start(bf16[1,2048,1,8]{1,3,2,0:T(8,128)(2,1)S(1)} %get-tuple-element.100) | copy-start | bytes 98308
  48.1 18.3 %copy-start.28 = (bf16[1,2048,1,8]{1,3,2,0:T(8,128)(2,1)}, bf16[1,2048,1,8]{1,3,2,0:T(8,128)(2,1)S(1)}, u32[]{:S(2)}) copy-start(bf16[1,2048,1,8]{1,3,2,0:T(8,128)(2,1)S(1)} %get-tuple-element.101) | copy-start | bytes 98308
  50.5 37.0 %copy-start.17 = (bf16[1,2048,64]{1,2,0:T(8,128)(2,1)}, bf16[1,2048,64]{1,2,0:T(8,128)(2,1)S(1)}, u32[]{:S(2)}) copy-start(bf16[1,2048,64]{1,2,0:T(8,128)(2,1)S(1)} %fusion.184) | copy-start | bytes 786436
  51.9 5.6 copy-start.11
  59.5 3.6 copy-start.1
  79.1 8.4 %copy-start.31 = (pred[512,512]{0,1:T(8,128)(4,1)S(1)}, pred[512,512]{0,1:T(8,128)(4,1)}, u32[]{:S(2)}) copy-start(pred[512,512]{0,1:T(8,128)(4,1)} %iota_compare_fusion.5) | copy-start | bytes 786436
  90.9 3.9 copy-start.20
  90.9 3.9 copy-start.41
  91.0 3.9 copy-start.43
  91.0 3.9 copy-start.61
  91.0 3.9 copy-start.62
  91.0 3.9 copy-start.63
  94.2 4.7 slice-start.5
  94.9 4.0 slice-start.6
  99.0 5.9 slice-start
  100.8 4.0 slice-start.1
  100.9 4.0 slice-start.2
  107.0 9.0 %copy-start.2 = (bf16[512,3,1536]{2,0,1:T(8,128)(2,1)}, bf16[512,3,1536]{2,0,1:T(8,128)(2,1)S(1)}, u32[]{:S(2)}) copy-start(bf16[512,3,1536]{2,0,1:T(8,128)(2,1)S(1)} %multiply_convert_fusion.1) | copy-start | bytes 14155780
  128.6 17.7 %copy-start.55 = (bf16[768,768]{1,0:T(8,128)(2,1)S(1)}, bf16[768,768]{1,0:T(8,128)(2,1)}, u32[]{:S(2)}) copy-start(bf16[768,768]{1,0:T(8,128)(2,1)} %param.31) | copy-start | bytes 3538948
  128.7 69.2 %reduce-scatter.11.cloned.1.call-start = ((), (), s32[]{:S(2)}) async-start(), calls=%async_computation.10 | async-start | bytes 3932160 | tf_op jit(solution)/shard_map/reduce_scatter | solution.py:224
  128.7 17.6 %copy-start.52 = (bf16[1,2048,768]{2,1,0:T(8,128)(2,1)S(1)}, bf16[1,2048,768]{2,1,0:T(8,128)(2,1)}, u32[]{:S(2)}) copy-start(bf16[1,2048,768]{2,1,0:T(8,128)(2,1)} %all-gather.8.cloned.1.call-done) | copy-start | bytes 9437188
  153.2 4.3 copy-start.18
  157.2 9.4 %slice-start.3 = ((s8[6291456]{0:T(1024)(128)(4,1)}), s8[2097152]{0:T(1024)(128)(4,1)S(1)}, s32[]{:S(2)}) async-start(s8[6291456]{0:T(1024)(128)(4,1)} %bitcast.269), calls=%async_computation.16 | async-start | bytes 4194304
  157.3 78.5 %reduce-scatter.7.cloned.1.call-start = ((), (), s32[]{:S(2)}) async-start(), calls=%async_computation.8 | async-start | bytes 3932160 | tf_op jit(solution)/shard_map/reduce_scatter | solution.py:221
  159.5 7.2 %slice-start.4 = ((s8[6291456]{0:T(1024)(128)(4,1)}), s8[4194304]{0:T(1024)(128)(4,1)S(1)}, s32[]{:S(2)}) async-start(s8[6291456]{0:T(1024)(128)(4,1)} %bitcast.269), calls=%async_computation.17 | async-start | bytes 8388608
  159.5 7.2 %copy-start.16 = (bf16[1,2048,1,48]{1,3,2,0:T(8,128)(2,1)S(1)}, bf16[1,2048,1,48]{1,3,2,0:T(8,128)(2,1)}, u32[]{:S(2)}) copy-start(bf16[1,2048,1,48]{1,3,2,0:T(8,128)(2,1)} %copy-done.15) | copy-start | bytes 589828
  159.5 7.2 %copy-start.27 = (bf16[1,2048,1,8]{1,3,2,0:T(8,128)(2,1)S(1)}, bf16[1,2048,1,8]{1,3,2,0:T(8,128)(2,1)}, u32[]{:S(2)}) copy-start(bf16[1,2048,1,8]{1,3,2,0:T(8,128)(2,1)} %copy-done.26) | copy-start | bytes 98308
  159.5 7.2 %copy-start.29 = (bf16[1,2048,1,8]{1,3,2,0:T(8,128)(2,1)S(1)}, bf16[1,2048,1,8]{1,3,2,0:T(8,128)(2,1)}, u32[]{:S(2)}) copy-start(bf16[1,2048,1,8]{1,3,2,0:T(8,128)(2,1)} %copy-done.28) | copy-start | bytes 98308
  171.7 111.3 %reduce-scatter.5.cloned.1.call-start = ((), (), s32[]{:S(2)}) async-start(), calls=%async_computation.6 | async-start | bytes 3932160 | tf_op jit(solution)/shard_map/reduce_scatter | solution.py:141
  171.8 5.0 copy-start.30
  171.8 5.0 copy-start.33
  171.8 5.0 copy-start.34
  171.8 5.0 copy-start.35
  171.8 5.0 copy-start.36
  179.5 230.5 %all-reduce.6.cloned.1.call-start = ((), (), s32[]{:S(2)}) async-start(), calls=%async_computation.11 | async-start | bytes 786432 | tf_op jit(solution)/shard_map/psum | solution.py:246
  179.8 3.7 copy-start.54
  179.8 3.8 copy-start.60
  183.6 4.2 copy-start.53
  183.6 4.2 copy-start.58
  187.8 4.2 copy-start.10
  194.1 41.7 %copy-start.9 = (bf16[1,512,768]{2,1,0:T(8,128)(2,1)S(1)}, bf16[1,512,768]{2,1,0:T(8,128)(2,1)}, u32[]{:S(2)}) copy-start(bf16[1,512,768]{2,1,0:T(8,128)(2,1)} %param.23) | copy-start | bytes 2359300
  194.1 41.7 %copy-start.39 = (f32[512]{0:T(512)S(1)}, f32[512]{0:T(512)}, u32[]{:S(2)}) copy-start(f32[512]{0:T(512)} %copy-done.38) | copy-start | bytes 6148
  194.1 41.7 %copy-start.45 = (f32[512]{0:T(512)S(1)}, f32[512]{0:T(512)}, u32[]{:S(2)}) copy-start(f32[512]{0:T(512)} %copy-done.44) | copy-start | bytes 6148
  194.1 41.7 %copy-start.46 = (f32[768]{0:T(1024)S(1)}, f32[768]{0:T(1024)}, u32[]{:S(2)}) copy-start(f32[768]{0:T(1024)} %param.32) | copy-start | bytes 9220
  194.1 41.7 %copy-start.47 = (f32[768]{0:T(1024)S(1)}, f32[768]{0:T(1024)}, u32[]{:S(2)}) copy-start(f32[768]{0:T(1024)} %param.34) | copy-start | bytes 9220
  194.1 422.5 %all-reduce.8.cloned.1.call-start = ((), (), s32[]{:S(2)}) async-start(), calls=%async_computation.12 | async-start | bytes 11796480 | tf_op jit(solution)/shard_map/psum | solution.py:243
  197.8 85.2 %copy-start.13 = (bf16[1,512,768]{2,1,0:T(8,128)(2,1)S(1)}, bf16[1,512,768]{2,1,0:T(8,128)(2,1)}, u32[]{:S(2)}) copy-start(bf16[1,512,768]{2,1,0:T(8,128)(2,1)} %param.24) | copy-start | bytes 2359300
  197.9 85.2 %copy-start.24 = (bf16[1,512,768]{2,1,0:T(8,128)(2,1)S(1)}, bf16[1,512,768]{2,1,0:T(8,128)(2,1)}, u32[]{:S(2)}) copy-start(bf16[1,512,768]{2,1,0:T(8,128)(2,1)} %reduce-scatter.11.cloned.1.call-done) | copy-start | bytes 2359300
  616.7 9.0 %copy-start.14 = (f32[768,768]{1,0:T(8,128)S(1)}, f32[768,768]{1,0:T(8,128)}, u32[]{:S(2)}) copy-start(f32[768,768]{1,0:T(8,128)} %get-tuple-element.140) | copy-start | bytes 7077892
  (16 other events, 31.0 us)
Sparse Core Ops, SparseCore 0:
  13.2 31.2 all-gather.3
  46.6 28.5 all-gather.7
  77.4 28.5 all-gather.5
  128.8 21.6 reduce-scatter.8
  157.4 37.9 reduce-scatter.10
  197.8 37.9 reduce-scatter.6
  238.5 38.1 reduce-scatter.4
  282.6 127.3 all-reduce.5
  415.1 201.4 all-reduce.7
where the time goes:
time: 640 us; the launch traced here: 634 us
  waiting for transfers between devices  392 us (61%)
  matrix products  132 us (21%)
  blocking collectives  40.1 us (6%)
  other arithmetic  33.5 us (5%)
  local copies, waits for them, and re-layouts  19.8 us (3%)
  between operations  16.1 us (3%)
    psum x1, waiting for transfers between devices, shards(): lax.psum((grad_query, grad_output, grad_upward, grad_downward), 'dp')  207 us
    psum x1, waiting for transfers between devices, shards(): lax.psum((grad_keyval, grad_gain_one, grad_bias_one, grad_gain_two, grad_...  123 us
    psum x1, blocking collectives, shards(): lax.psum((grad_keyval, grad_gain_one, grad_bias_one, grad_gain_two, grad_...  40.1 us
    reduce_scatter x1, waiting for transfers between devices, shards(): lax.psum_scatter(norm_part_one.astype(jnp.bfloat16), 'tp', scatter_dimens...  37.9 us
    all_gather x1, waiting for transfers between devices, shards(): lax.all_gather(low_one, 'tp', axis=1, tiled=True)  23.4 us
    dot_general x5, matrix products, against(): lax.dot_general(left, weight, (((2,), (1,)), ((), ())), preferred_element...  19.8 us
    unnamed x147, local copies, waits for them, and re-layouts  19.6 us
    dot_general x5, matrix products, outer_sum(): lax.dot_general(left, right, (((0, 1), (0, 1)), ((), ())), preferred_elem...  17.6 us
  transfers between devices with their start and end apart: 9, of which 4 were waited for; matrix products, arithmetic and copies ran while one was open for 25% of the time, Pallas kernels for 0%

commit v1 on v0

--- a/solution.py
+++ b/solution.py
@@ -244,7 +244,8 @@
         (grad_query, grad_output, grad_upward, grad_downward), "dp"
     )
     grad_keyval, grad_gain_one, grad_bias_one, grad_gain_two, grad_bias_two = lax.psum(
-        (grad_keyval, grad_gain_one, grad_bias_one, grad_gain_two, grad_bias_two), ("dp", "tp")
+        lax.psum((grad_keyval, grad_gain_one, grad_bias_one, grad_gain_two, grad_bias_two), "tp"),
+        "dp",
     )
     return (
         block_out,

time: 640 us -> 553 us (0.86)
  waiting for transfers between devices: 392 us -> 295 us
  blocking collectives: 40.1 us -> 49.2 us
    psum x1, waiting for transfers between devices: 123 us -> 0.02 us  [shards(): lax.psum((grad_keyval, grad_gain_one, grad_bias_one, grad_gain_two, grad_...]
    psum x0 -> x1, blocking collectives: none -> 37.8 us  [shards(): lax.psum(lax.psum((grad_keyval, grad_gain_one, grad_bias_one, grad_gain_t...]
    psum x1, blocking collectives: 40.1 us -> 11.3 us  [shards(): lax.psum((grad_keyval, grad_gain_one, grad_bias_one, grad_gain_two, grad_...]
    reduce_scatter x1, waiting for transfers between devices: 0.02 us -> 28.8 us  [shards(): lax.psum_scatter(norm_part_two.astype(jnp.bfloat16), 'tp', scatter_dimens...]
    unnamed x147 -> x145, local copies, waits for them, and re-layouts: 19.6 us -> 17.7 us
  transfers between devices with their start and end apart: 9 -> 9, of which waited for: 4 -> 4; matrix products, arithmetic and copies ran while one was open for 25% -> 29% of each run, Pallas kernels for 0% -> 0%
where the time goes in v1:
time: 553 us; the launch traced here: 548 us
  waiting for transfers between devices  295 us (53%)
  matrix products  135 us (24%)
  blocking collectives  49.2 us (9%)
  other arithmetic  33.5 us (6%)
  local copies, waits for them, and re-layouts  17.9 us (3%)
  between operations  16 us (3%)
    psum x1, waiting for transfers between devices, shards(): lax.psum((grad_query, grad_output, grad_upward, grad_downward), 'dp')  202 us
    reduce_scatter x1, waiting for transfers between devices, shards(): lax.psum_scatter(norm_part_one.astype(jnp.bfloat16), 'tp', scatter_dimens...  40.6 us
    psum x1, blocking collectives, shards(): lax.psum(lax.psum((grad_keyval, grad_gain_one, grad_bias_one, grad_gain_t...  37.8 us
    reduce_scatter x1, waiting for transfers between devices, shards(): lax.psum_scatter(norm_part_two.astype(jnp.bfloat16), 'tp', scatter_dimens...  28.8 us
    all_gather x1, waiting for transfers between devices, shards(): lax.all_gather(low_one, 'tp', axis=1, tiled=True)  23.4 us
    dot_general x5, matrix products, against(): lax.dot_general(left, weight, (((2,), (1,)), ((), ())), preferred_element...  23 us
    unnamed x145, local copies, waits for them, and re-layouts  17.7 us
    dot_general x1, matrix products, shards(): jnp.dot(rows_two, up_weight, preferred_element_type=jnp.float32)  17.5 us
  transfers between devices with their start and end apart: 9, of which 4 were waited for; matrix products, arithmetic and copies ran while one was open for 29% of the time, Pallas kernels for 0%

profile of v1, /device:TPU:0, one launch (start us, length us, event | category | flops | bytes accessed | tf_op | source)
XLA Modules:
  0.0 547.7 jit_solution(8053667522698123851)
XLA Ops:
  7.3 1.4 convert_reduce_fusion.1
  8.7 1.5 fusion.101
  10.2 2.9 fusion.89
  14.4 1.6 fusion.110
  16.9 0.8 iota_compare_fusion.5
  18.1 1.4 iota_compare_fusion.1
  20.1 0.9 broadcast_multiply_fusion
  21.1 23.4 %all-gather.4.cloned.1.call-done = bf16[1,2048,768]{2,1,0:T(8,128)(2,1)} async-done(((bf16[1,512,768]{2,1,0:T(8,128)(2,1)}), bf16[1,2048,768]{2,1,0:T(8,128)(2,1)}) %all-gather.4.cloned.1.call-update) | async-done | bytes 3145744 | tf_op jit(solution)/shard_map/all_gather | solution.py:87
  44.5 3.2 fusion.186
  48.2 2.1 fusion.58
  50.6 1.3 fusion.31
  51.9 2.1 fusion.25
  54.6 2.9 fusion.190
  57.5 2.0 fusion.187
  59.5 1.4 fusion.2
  60.9 2.2 copy-done.1
  63.1 2.8 fusion.189
  66.5 5.9 %fusion.4 = (f32[512,3]{0,1:T(4,128)S(1)}, f32[512,3,2048]{2,0,1:T(8,128)}) fusion(pred[512,2048]{1,0:T(8,128)(4,1)S(1)} %iota_compare_fusion, bf16[1,2048,1,48]{1,3,2,0:T(8,128)(2,1)S(1)} %slice.370, bf16[1,2048,1,8]{1,3,2,0:T(8,128)(2,1)S(1)} %get-tuple-element.106, bf16[1,2048,1,8]{1,3,2,0:T(8,128)(2,1)S(1)} %get-tuple-element.105, ...), kind=kOutput, calls=%fused_computation.16 | convolution fusion | flops 412875264 | bytes 14096384 | tf_op jit(solution)/shard_map/sqhd,skd->sqhk/dot_general | solution.py:105
  72.3 6.7 %fusion = f32[512,3]{0,1:T(4,128)S(1)} fusion(f32[512,3,2048]{2,0,1:T(8,128)} %get-tuple-element.119, f32[512,3]{0,1:T(4,128)S(1)} %get-tuple-element.118, pred[512,2048]{1,0:T(8,128)(4,1)S(1)} %iota_compare_fusion), kind=kLoop, calls=%fused_computation.5 | loop fusion | flops 12581376 | bytes 13643776 | tf_op jit(solution)/shard_map/reduce_sum | solution.py:124
  79.1 7.8 %fusion.188 = (bf16[512,3,64]{0,2,1:T(8,128)(2,1)}, f32[512,3,64]{0,2,1:T(8,128)}) fusion(bf16[1,2048,128]{1,2,0:T(8,128)(2,1)S(1)} %get-tuple-element.112, f32[512,3,2048]{2,0,1:T(8,128)} %get-tuple-element.119, f32[512,3]{0,1:T(4,128)S(1)} %fusion, f32[512,3]{0,1:T(4,128)S(1)} %get-tuple-element.118, pred[512,2048]{1,0:T(8,128)(4,1)S(1)} %iota_compare_fusion), kind=kOutput, calls=%fused_computation.286 | convolution fusion | flops 418480128 | bytes 14499840 | tf_op jit(solution)/shard_map/sqhk,skd->sqhd/dot_general | solution.py:127
  88.3 1.6 copy-done.3
  91.0 3.2 fusion.61
  95.0 1.4 fusion.133
  96.4 0.8 multiply_convert_fusion.3
  97.3 1.1 copy-done.7
  99.0 1.9 fusion.116
  100.9 2.4 multiply_convert_fusion.2
  104.1 0.8 copy-done.6
  104.9 2.1 multiply_convert_fusion.1
  107.1 8.8 %multiply_convert_fusion = bf16[512,3,2048]{2,0,1:T(8,128)(2,1)S(1)} fusion(f32[512,3,2048]{2,0,1:T(8,128)} %get-tuple-element.119, f32[512,3]{0,1:T(4,128)S(1)} %get-tuple-element.80, f32[512,3]{0,1:T(4,128)S(1)} %copy-done.48, pred[512,2048]{1,0:T(8,128)(4,1)S(1)} %iota_compare_fusion, bf16[1,2048,128]{1,2,0:T(8,128)(2,1)S(1)} %copy-done.20, ...), kind=kOutput, calls=%fused_computation | convolution fusion | flops 421527552 | bytes 20398080 | tf_op jit(solution)/shard_map/sqhd,skd->sqhk/dot_general | solution.py:176
  116.1 0.9 fusion.76
  117.0 1.2 fusion.74
  118.5 1.6 fusion.67
  120.4 6.4 %fusion.70 = f32[1,2048,64]{1,2,0:T(8,128)S(1)} fusion(f32[512,3,2048]{2,0,1:T(8,128)} %get-tuple-element.119, f32[512,3]{0,1:T(4,128)S(1)} %copy-done.48, pred[512,2048]{1,0:T(8,128)(4,1)S(1)} %iota_compare_fusion, bf16[1,2048,3,64]{1,3,2,0:T(8,128)(2,1)S(1)} %bitcast.283), kind=kOutput, calls=%fused_computation.100 | convolution fusion | flops 415236096 | bytes 14360576 | tf_op jit(solution)/shard_map/sqhk,sqhd->skd/dot_general | solution.py:201
  127.8 0.8 pad_maximum_fusion.2
  128.8 17.5 %fusion.7 = (bf16[2048,768]{1,0:T(8,128)(2,1)}, f32[2048,768]{1,0:T(8,128)S(1)}) fusion(bf16[768,768]{1,0:T(8,128)(2,1)S(1)} %copy-done, bf16[1,2048,768]{2,1,0:T(8,128)(2,1)} %all-gather.6.cloned.1.call-done), kind=kOutput, calls=%fused_computation.19 | convolution fusion | flops 2518155264 | bytes 13762560 | tf_op jit(solution)/shard_map/dot_general | solution.py:138
  146.3 6.2 %fusion.13 = bf16[2048,768]{1,0:T(8,128)(2,1)} fusion(f32[2048,768]{1,0:T(8,128)S(1)} %get-tuple-element.123, bf16[768,768]{1,0:T(8,128)(2,1)S(1)} %copy-done.55, bf16[1,2048,768]{2,1,0:T(8,128)(2,1)S(1)} %copy-done.52), kind=kOutput, calls=%fused_computation.25 | convolution fusion | flops 2431647744 | bytes 13762560 | tf_op jit(solution)/shard_map/dot_general | solution.py:54
  152.5 2.1 fusion.127
  154.8 6.2 %fusion.54 = bf16[1,2048,768]{2,1,0:T(8,128)(2,1)} fusion(bf16[2048,768]{1,0:T(8,128)(2,1)} %fusion.13, bf16[768,768]{1,0:T(8,128)(2,1)S(1)} %copy-done), kind=kOutput, calls=%fused_computation.86 | convolution fusion | flops 2417491968 | bytes 7471104 | tf_op jit(solution)/shard_map/dot_general | solution.py:54
  161.2 1.9 fusion.113
  163.2 3.1 fusion.112
  166.3 3.9 fusion.115
  170.3 2.0 fusion.114
  172.5 2.7 fusion.53
  175.4 5.0 fusion.191
  180.4 2.7 fusion.55
  183.4 3.6 fusion.47
  187.0 3.5 fusion.34
  190.5 4.2 fusion.39
  194.7 4.2 fusion.32
  199.0 28.8 %reduce-scatter.11.cloned.1.call-done = bf16[1,512,768]{2,1,0:T(8,128)(2,1)} async-done(((bf16[1,2048,768]{2,1,0:T(8,128)(2,1)}), bf16[1,512,768]{2,1,0:T(8,128)(2,1)}) %reduce-scatter.11.cloned.1.call-update) | async-done | bytes 786448 | tf_op jit(solution)/shard_map/reduce_scatter | solution.py:224
  227.7 40.6 %reduce-scatter.7.cloned.1.call-done = bf16[1,512,768]{2,1,0:T(8,128)(2,1)} async-done(((bf16[1,2048,768]{2,1,0:T(8,128)(2,1)}), bf16[1,512,768]{2,1,0:T(8,128)(2,1)}) %reduce-scatter.7.cloned.1.call-update) | async-done | bytes 786448 | tf_op jit(solution)/shard_map/reduce_scatter | solution.py:221
  268.4 4.6 fusion.100
  273.0 11.3 %all-reduce.3 = (f32[768]{0:T(1024)}, f32[768]{0:T(1024)}, f32[768]{0:T(1024)}, f32[768]{0:T(1024)}) all-reduce(f32[768]{0:T(1024)} %get-tuple-element.67, f32[768]{0:T(1024)} %get-tuple-element.72, f32[768]{0:T(1024)} %get-tuple-element.74, f32[768]{0:T(1024)} %get-tuple-element.76), channel_id=1, replica_groups=mesh['dp'=8,'tp'=4] {'tp'}, use_global_device_ids=true, to_apply=%region_30.31 | all-reduce | flops 3072 | bytes 24576 | tf_op jit(solution)/shard_map/psum | solution.py:247
  284.4 37.8 %all-reduce.1 = (f32[768]{0:T(1024)}, f32[768]{0:T(1024)}, f32[768]{0:T(1024)}, f32[768]{0:T(1024)}) all-reduce(f32[768]{0:T(1024)} %get-tuple-element.90, f32[768]{0:T(1024)} %get-tuple-element.91, f32[768]{0:T(1024)} %get-tuple-element.92, f32[768]{0:T(1024)} %get-tuple-element.93), channel_id=1, replica_groups=mesh['dp'=8,'tp'=4] {'dp'}, use_global_device_ids=true, to_apply=%region_31.32 | all-reduce | flops 3072 | bytes 24576 | tf_op jit(solution)/shard_map/psum | solution.py:246
  322.2 1.3 broadcast_multiply_fusion.1
  323.5 1.3 broadcast_multiply_fusion.3
  324.7 4.0 fusion.97
  328.7 201.6 %all-reduce.9.cloned.1.call-done = (f32[768,192]{0,1:T(8,128)}, f32[768,128]{1,0:T(8,128)}, f32[192,768]{1,0:T(8,128)}, f32[768,768]{1,0:T(8,128)}, f32[768,768]{1,0:T(8,128)}) async-done(((f32[768,192]{0,1:T(8,128)}, f32[768,128]{1,0:T(8,128)}, f32[192,768]{1,0:T(8,128)}, f32[768,768]{1,0:T(8,128)}, f32[768,768]{1,0:T(8,128)}), (f32[768,192]{0,1:T(8,128)}, f32[768,128]{1,0:T(8,128)}, f32[192,768]{1,0:T(8,128)}, ...) | async-done | bytes 6291472 | tf_op jit(solution)/shard_map/psum | solution.py:243
  530.4 2.1 copy.43
  532.4 1.8 copy.44
  534.2 1.9 copy.45
  536.1 3.2 copy.46
  539.3 1.4 copy.47
  (200 shorter events, 11.6 us)
Async XLA Ops:
  7.2 121.6 %copy-start = (bf16[768,768]{1,0:T(8,128)(2,1)S(1)}, bf16[768,768]{1,0:T(8,128)(2,1)}, u32[]{:S(2)}) copy-start(bf16[768,768]{1,0:T(8,128)(2,1)} %param.30) | copy-start | bytes 3538948
  7.2 6.6 %copy-start.57 = (f32[8]{0:T(128)S(1)}, f32[8]{0:T(128)}, u32[]{:S(2)}) copy-start(f32[8]{0:T(128)} %param.26) | copy-start | bytes 100
  7.2 7.2 %copy-start.12 = (bf16[1,512,768]{2,1,0:T(8,128)(2,1)S(1)}, bf16[1,512,768]{2,1,0:T(8,128)(2,1)}, u32[]{:S(2)}) copy-start(bf16[1,512,768]{2,1,0:T(8,128)(2,1)} %param.24) | copy-start | bytes 2359300
  7.2 37.3 %all-gather.4.cloned.1.call-start = ((), (), s32[]{:S(2)}) async-start(), calls=%async_computation.4 | async-start | bytes 3932160 | tf_op jit(solution)/shard_map/all_gather | solution.py:87
  8.7 9.4 %copy-start.38 = (f32[512]{0:T(512)}, f32[512]{0:T(512)S(1)}, u32[]{:S(2)}) copy-start(f32[512]{0:T(512)S(1)} %broadcast_multiply_fusion.5) | copy-start | bytes 6148
  10.2 34.3 %copy-start.32 = (bf16[768,128]{1,0:T(8,128)(2,1)S(1)}, bf16[768,128]{1,0:T(8,128)(2,1)}, u32[]{:S(2)}) copy-start(bf16[768,128]{1,0:T(8,128)(2,1)} %param.28) | copy-start | bytes 589828
  10.2 7.8 %copy-start.44 = (f32[512]{0:T(512)}, f32[512]{0:T(512)S(1)}, u32[]{:S(2)}) copy-start(f32[512]{0:T(512)S(1)} %add_rsqrt_fusion) | copy-start | bytes 6148
  13.1 77.8 %all-gather.8.cloned.1.call-start = ((), (), s32[]{:S(2)}) async-start(), calls=%async_computation.7 | async-start | bytes 3932160 | tf_op jit(solution)/shard_map/all_gather | solution.py:153
  16.1 112.7 %all-gather.6.cloned.1.call-start = ((), (), s32[]{:S(2)}) async-start(), calls=%async_computation.5 | async-start | bytes 3932160 | tf_op jit(solution)/shard_map/all_gather | solution.py:88
  16.8 135.7 %reduce-scatter.9.cloned.1.call-start = ((), (), s32[]{:S(2)}) async-start(), calls=%async_computation.9 | async-start | bytes 655360 | tf_op jit(solution)/shard_map/reduce_scatter | solution.py:227
  16.9 33.4 %copy-start.50 = (f32[8]{0:T(128)}, f32[8]{0:T(128)S(1)}, u32[]{:S(2)}) copy-start(f32[8]{0:T(128)S(1)} %multiply_power_fusion) | copy-start | bytes 100
  21.1 29.3 %copy-start.21 = (f32[2048,8]{0,1:T(8,128)}, f32[2048,8]{0,1:T(8,128)S(1)}, u32[]{:S(2)}) copy-start(f32[2048,8]{0,1:T(8,128)S(1)} %get-tuple-element.109) | copy-start | bytes 196612
  44.5 3.6 copy-start.8
  47.7 31.4 %copy-start.19 = (bf16[1,2048,128]{1,2,0:T(8,128)(2,1)}, bf16[1,2048,128]{1,2,0:T(8,128)(2,1)S(1)}, u32[]{:S(2)}) copy-start(bf16[1,2048,128]{1,2,0:T(8,128)(2,1)S(1)} %get-tuple-element.112) | copy-start | bytes 1572868
  47.8 18.7 %copy-start.15 = (bf16[1,2048,1,48]{1,3,2,0:T(8,128)(2,1)}, bf16[1,2048,1,48]{1,3,2,0:T(8,128)(2,1)S(1)}, u32[]{:S(2)}) copy-start(bf16[1,2048,1,48]{1,3,2,0:T(8,128)(2,1)S(1)} %slice.370) | copy-start | bytes 589828
  48.1 18.3 %copy-start.26 = (bf16[1,2048,1,8]{1,3,2,0:T(8,128)(2,1)}, bf16[1,2048,1,8]{1,3,2,0:T(8,128)(2,1)S(1)}, u32[]{:S(2)}) copy-start(bf16[1,2048,1,8]{1,3,2,0:T(8,128)(2,1)S(1)} %get-tuple-element.105) | copy-start | bytes 98308
  48.1 18.3 %copy-start.28 = (bf16[1,2048,1,8]{1,3,2,0:T(8,128)(2,1)}, bf16[1,2048,1,8]{1,3,2,0:T(8,128)(2,1)S(1)}, u32[]{:S(2)}) copy-start(bf16[1,2048,1,8]{1,3,2,0:T(8,128)(2,1)S(1)} %get-tuple-element.106) | copy-start | bytes 98308
  50.5 37.1 %copy-start.17 = (bf16[1,2048,64]{1,2,0:T(8,128)(2,1)}, bf16[1,2048,64]{1,2,0:T(8,128)(2,1)S(1)}, u32[]{:S(2)}) copy-start(bf16[1,2048,64]{1,2,0:T(8,128)(2,1)S(1)} %fusion.184) | copy-start | bytes 786436
  51.9 5.6 %copy-start.11 = (f32[512,3,1024]{2,0,1:T(8,128)}, f32[512,3,1024]{2,0,1:T(8,128)S(1)}, u32[]{:S(2)}) copy-start(f32[512,3,1024]{2,0,1:T(8,128)S(1)} %get-tuple-element.115) | copy-start | bytes 18874372
  59.5 3.6 copy-start.1
  79.1 8.5 %copy-start.31 = (pred[512,512]{0,1:T(8,128)(4,1)S(1)}, pred[512,512]{0,1:T(8,128)(4,1)}, u32[]{:S(2)}) copy-start(pred[512,512]{0,1:T(8,128)(4,1)} %iota_compare_fusion.5) | copy-start | bytes 786436
  91.0 3.9 copy-start.20
  91.0 3.9 copy-start.41
  91.0 3.9 copy-start.43
  91.0 3.9 copy-start.60
  91.0 3.9 copy-start.61
  91.0 3.9 copy-start.62
  94.3 4.7 slice-start.5
  95.0 4.0 slice-start.6
  99.0 5.9 %slice-start = ((s8[9437184]{0:T(1024)(128)(4,1)}), s8[4194304]{0:T(1024)(128)(4,1)S(1)}, s32[]{:S(2)}) async-start(s8[9437184]{0:T(1024)(128)(4,1)} %bitcast.267), calls=%async_computation.13 | async-start | bytes 8388608
  100.9 4.0 slice-start.1
  100.9 4.0 slice-start.2
  107.1 9.0 %copy-start.2 = (bf16[512,3,1536]{2,0,1:T(8,128)(2,1)}, bf16[512,3,1536]{2,0,1:T(8,128)(2,1)S(1)}, u32[]{:S(2)}) copy-start(bf16[512,3,1536]{2,0,1:T(8,128)(2,1)S(1)} %multiply_convert_fusion.1) | copy-start | bytes 14155780
  128.7 17.6 %copy-start.55 = (bf16[768,768]{1,0:T(8,128)(2,1)S(1)}, bf16[768,768]{1,0:T(8,128)(2,1)}, u32[]{:S(2)}) copy-start(bf16[768,768]{1,0:T(8,128)(2,1)} %param.31) | copy-start | bytes 3538948
  128.7 70.3 %all-reduce.7.cloned.1.call-start = ((), (), s32[]{:S(2)}) async-start(), calls=%async_computation.11 | async-start | bytes 786432 | tf_op jit(solution)/shard_map/psum | solution.py:247
  128.8 17.5 %copy-start.52 = (bf16[1,2048,768]{2,1,0:T(8,128)(2,1)S(1)}, bf16[1,2048,768]{2,1,0:T(8,128)(2,1)}, u32[]{:S(2)}) copy-start(bf16[1,2048,768]{2,1,0:T(8,128)(2,1)} %all-gather.8.cloned.1.call-done) | copy-start | bytes 9437188
  146.3 6.2 %copy-start.10 = (bf16[1,512,768]{2,1,0:T(8,128)(2,1)S(1)}, bf16[1,512,768]{2,1,0:T(8,128)(2,1)}, u32[]{:S(2)}) copy-start(bf16[1,512,768]{2,1,0:T(8,128)(2,1)} %get-tuple-element.99) | copy-start | bytes 2359300
  154.6 6.6 %copy-start.18 = (bf16[1,2048,64]{1,2,0:T(8,128)(2,1)S(1)}, bf16[1,2048,64]{1,2,0:T(8,128)(2,1)}, u32[]{:S(2)}) copy-start(bf16[1,2048,64]{1,2,0:T(8,128)(2,1)} %copy-done.17) | copy-start | bytes 786436
  154.6 73.2 %reduce-scatter.11.cloned.1.call-start = ((), (), s32[]{:S(2)}) async-start(), calls=%async_computation.10 | async-start | bytes 3932160 | tf_op jit(solution)/shard_map/reduce_scatter | solution.py:224
  161.1 9.1 %slice-start.3 = ((s8[6291456]{0:T(1024)(128)(4,1)}), s8[2097152]{0:T(1024)(128)(4,1)S(1)}, s32[]{:S(2)}) async-start(s8[6291456]{0:T(1024)(128)(4,1)} %bitcast.269), calls=%async_computation.16 | async-start | bytes 4194304
  161.1 107.3 %reduce-scatter.7.cloned.1.call-start = ((), (), s32[]{:S(2)}) async-start(), calls=%async_computation.8 | async-start | bytes 3932160 | tf_op jit(solution)/shard_map/reduce_scatter | solution.py:221
  163.1 7.1 %slice-start.4 = ((s8[6291456]{0:T(1024)(128)(4,1)}), s8[4194304]{0:T(1024)(128)(4,1)S(1)}, s32[]{:S(2)}) async-start(s8[6291456]{0:T(1024)(128)(4,1)} %bitcast.269), calls=%async_computation.17 | async-start | bytes 8388608
  163.1 7.1 %copy-start.16 = (bf16[1,2048,1,48]{1,3,2,0:T(8,128)(2,1)S(1)}, bf16[1,2048,1,48]{1,3,2,0:T(8,128)(2,1)}, u32[]{:S(2)}) copy-start(bf16[1,2048,1,48]{1,3,2,0:T(8,128)(2,1)} %copy-done.15) | copy-start | bytes 589828
  163.1 7.1 %copy-start.27 = (bf16[1,2048,1,8]{1,3,2,0:T(8,128)(2,1)S(1)}, bf16[1,2048,1,8]{1,3,2,0:T(8,128)(2,1)}, u32[]{:S(2)}) copy-start(bf16[1,2048,1,8]{1,3,2,0:T(8,128)(2,1)} %copy-done.26) | copy-start | bytes 98308
  163.1 7.1 %copy-start.29 = (bf16[1,2048,1,8]{1,3,2,0:T(8,128)(2,1)S(1)}, bf16[1,2048,1,8]{1,3,2,0:T(8,128)(2,1)}, u32[]{:S(2)}) copy-start(bf16[1,2048,1,8]{1,3,2,0:T(8,128)(2,1)} %copy-done.28) | copy-start | bytes 98308
  175.2 149.5 %reduce-scatter.5.cloned.1.call-start = ((), (), s32[]{:S(2)}) async-start(), calls=%async_computation.6 | async-start | bytes 3932160 | tf_op jit(solution)/shard_map/reduce_scatter | solution.py:141
  175.3 5.0 copy-start.30
  175.3 5.0 copy-start.33
  175.3 5.0 copy-start.34
  175.3 5.0 copy-start.35
  175.3 5.0 copy-start.36
  183.1 347.3 %all-reduce.9.cloned.1.call-start = ((), (), s32[]{:S(2)}) async-start(), calls=%async_computation.12 | async-start | bytes 12582912 | tf_op jit(solution)/shard_map/psum | solution.py:243
  183.4 7.1 %copy-start.54 = (bf16[1,2048,768]{2,1,0:T(8,128)(2,1)S(1)}, bf16[1,2048,768]{2,1,0:T(8,128)(2,1)}, u32[]{:S(2)}) copy-start(bf16[1,2048,768]{2,1,0:T(8,128)(2,1)} %all-gather.6.cloned.1.call-done) | copy-start | bytes 9437188
  183.4 7.1 %copy-start.59 = (bf16[2048,768]{1,0:T(8,128)(2,1)S(1)}, bf16[2048,768]{1,0:T(8,128)(2,1)}, u32[]{:S(2)}) copy-start(bf16[2048,768]{1,0:T(8,128)(2,1)} %fusion.13) | copy-start | bytes 9437188
  190.5 4.2 copy-start.53
  190.5 4.2 copy-start.58
  198.9 69.5 %copy-start.9 = (bf16[1,512,768]{2,1,0:T(8,128)(2,1)S(1)}, bf16[1,512,768]{2,1,0:T(8,128)(2,1)}, u32[]{:S(2)}) copy-start(bf16[1,512,768]{2,1,0:T(8,128)(2,1)} %param.23) | copy-start | bytes 2359300
  198.9 69.5 %copy-start.39 = (f32[512]{0:T(512)S(1)}, f32[512]{0:T(512)}, u32[]{:S(2)}) copy-start(f32[512]{0:T(512)} %copy-done.38) | copy-start | bytes 6148
  198.9 69.5 %copy-start.45 = (f32[512]{0:T(512)S(1)}, f32[512]{0:T(512)}, u32[]{:S(2)}) copy-start(f32[512]{0:T(512)} %copy-done.44) | copy-start | bytes 6148
  198.9 69.5 %copy-start.46 = (f32[768]{0:T(1024)S(1)}, f32[768]{0:T(1024)}, u32[]{:S(2)}) copy-start(f32[768]{0:T(1024)} %param.32) | copy-start | bytes 9220
  198.9 69.5 %copy-start.47 = (f32[768]{0:T(1024)S(1)}, f32[768]{0:T(1024)}, u32[]{:S(2)}) copy-start(f32[768]{0:T(1024)} %param.34) | copy-start | bytes 9220
  199.0 125.8 %copy-start.13 = (bf16[1,512,768]{2,1,0:T(8,128)(2,1)S(1)}, bf16[1,512,768]{2,1,0:T(8,128)(2,1)}, u32[]{:S(2)}) copy-start(bf16[1,512,768]{2,1,0:T(8,128)(2,1)} %param.24) | copy-start | bytes 2359300
  227.7 97.0 %copy-start.24 = (bf16[1,512,768]{2,1,0:T(8,128)(2,1)S(1)}, bf16[1,512,768]{2,1,0:T(8,128)(2,1)}, u32[]{:S(2)}) copy-start(bf16[1,512,768]{2,1,0:T(8,128)(2,1)} %reduce-scatter.11.cloned.1.call-done) | copy-start | bytes 2359300
  530.4 9.0 %copy-start.14 = (f32[768,768]{1,0:T(8,128)S(1)}, f32[768,768]{1,0:T(8,128)}, u32[]{:S(2)}) copy-start(f32[768,768]{1,0:T(8,128)} %get-tuple-element.145) | copy-start | bytes 7077892
  (15 other events, 29.2 us)
Sparse Core Ops, SparseCore 0:
  13.2 31.2 all-gather.3
  46.6 28.5 all-gather.7
  77.4 28.5 all-gather.5
  128.8 21.6 reduce-scatter.8
  154.7 32.6 all-reduce.6
  189.8 37.9 reduce-scatter.10
  230.4 37.9 reduce-scatter.6
  270.9 37.9 reduce-scatter.4
  315.1 215.2 all-reduce.8
